TPU v7x, 32 devices: a whole 2x2x4 slice. The times are simulated.
32 devices in a mesh: dp: 2 (over x), row: 4 (over y, core), col: 4 (over z).
Axes of the slice: x: 2, y: 2, z: 4, core: 2. Of those that a mesh axis runs over, the one named last changes fastest.
Arguments:
- tokens_in: bfloat16 [16384, 1024], P(('dp', 'col'), 'row'), may hold values from -6 to 6
- cotangent: bfloat16 [16384, 1024], P(('dp', 'col'), 'row'), may hold values from -6 to 6
- doc_lengths: int32 [8, 6], P(('dp', 'row')), may hold values from 1 to 1024, 2048 in all within a row
- mixer_gain: bfloat16 [1024], P('row'), may hold values from 0.099609375 to 1.8984375
- w_query: bfloat16 [1024, 512], P('row', 'col'), may hold values from -0.1875 to 0.1875
- w_key: bfloat16 [1024, 512], P('row', 'col'), may hold values from -0.1875 to 0.1875
- w_value: bfloat16 [1024, 1024], P('row', 'col'), may hold values from -0.1875 to 0.1875
- w_outgate: bfloat16 [1024, 1024], P('row', 'col'), may hold values from -0.1875 to 0.1875
- w_rank_in: bfloat16 [1024, 16], P('row'), may hold values from -0.1875 to 0.1875
- w_rank_out: bfloat16 [16, 512], P(None, 'col'), may hold values from -1.5 to 1.5
- decay_bias: bfloat16 [512], P('col'), may hold values from -1 to 6
- head_gain: bfloat16 [256], replicated, may hold values from 0.099609375 to 1.8984375
- w_output: bfloat16 [1024, 1024], P('col', 'row'), may hold values from -0.1875 to 0.1875
- ffn_gain: bfloat16 [1024], P('row'), may hold values from 0.099609375 to 1.8984375
- w_gate: bfloat16 [1024, 2816], P('row', 'col'), may hold values from -0.1875 to 0.1875
- w_up: bfloat16 [1024, 2816], P('row', 'col'), may hold values from -0.1875 to 0.1875
- w_down: bfloat16 [2816, 1024], P('col', 'row'), may hold values from -0.109375 to 0.109375
Outputs:
- output_rows: bfloat16 [16384, 1024], P(('dp', 'col'), 'row')
- grad_tokens: float32 [16384, 1024], P(('dp', 'col'), 'row')
- grad_mixer_gain: float32 [1024], P('row')
- grad_w_query: float32 [1024, 512], P('row', 'col')
- grad_w_key: float32 [1024, 512], P('row', 'col')
- grad_w_value: float32 [1024, 1024], P('row', 'col')
- grad_w_outgate: float32 [1024, 1024], P('row', 'col')
- grad_w_rank_in: float32 [1024, 16], P('row')
- grad_w_rank_out: float32 [16, 512], P(None, 'col')
- grad_decay_bias: float32 [512], P('col')
- grad_head_gain: float32 [256], replicated
- grad_w_output: float32 [1024, 1024], P('col', 'row')
- grad_ffn_gain: float32 [1024], P('row')
- grad_w_gate: float32 [1024, 2816], P('row', 'col')
- grad_w_up: float32 [1024, 2816], P('row', 'col')
- grad_w_down: float32 [2816, 1024], P('col', 'row')
Inputs may be any that keep to these rules, and one draw needn't show every extreme that they name: `doc_lengths`: each row sums to 2048.
All inputs are finite; a program needn't handle non-finite values.
Results may differ from a plain program's by a relative error of at most 0.015.
Values may be sent and summed in bfloat16 or wider, within the bound.
No kernel may reach another device: no remote copies, remote signals or barrier semaphores. Data moves between devices by JAX's collectives and lax.ppermute only.
A program may use at most 256 MiB of HBM per device.

v0:
```python
from functools import partial
import jax
import jax.numpy as jnp
from jax import lax
from jax.sharding import PartitionSpec as P

D = 1024
DK = 512
SEQ_LEN = 2048
SPAN = 64
HK = 128
HV = 256
exact_mode = lax.Precision.HIGHEST
norm_eps = 1e-05
head_eps = 1.0
contract_rows = (((0,), (0,)), ((), ()))
contract_cols = (((1,), (1,)), ((), ()))


def product(left, right):
    return jnp.dot(left, right, preferred_element_type=jnp.float32)


def gram_of(left, right):
    return lax.dot_general(left, right, contract_rows, preferred_element_type=jnp.float32)


def times_transpose(left, weight):
    return lax.dot_general(left, weight, contract_cols, preferred_element_type=jnp.float32)


def feature_sum(vector):
    return lax.psum(vector, "row")


def col_tokens(block):
    return lax.all_gather(block, "col", axis=0, tiled=True)


def col_parts(partial_sum):
    return lax.psum_scatter(partial_sum, "col", scatter_dimension=0, tiled=True)


def data_sum(group):
    return (
        lax.psum(group[0].astype(jnp.bfloat16), "dp").astype(jnp.float32),
        lax.psum(group[1].astype(jnp.bfloat16), "dp").astype(jnp.float32),
        lax.psum(group[2].astype(jnp.bfloat16), "dp").astype(jnp.float32),
        lax.psum(group[3].astype(jnp.bfloat16), "dp").astype(jnp.float32),
        lax.psum(group[4].astype(jnp.bfloat16), "dp").astype(jnp.float32),
        lax.psum(group[5].astype(jnp.bfloat16), "dp").astype(jnp.float32),
        lax.psum(group[6].astype(jnp.bfloat16), "dp").astype(jnp.float32),
        lax.psum(group[7].astype(jnp.bfloat16), "dp").astype(jnp.float32),
    )


def segment_ids(doc_lengths, length):
    starts = jnp.cumsum(doc_lengths, axis=-1, dtype=jnp.int32) - doc_lengths
    places = jnp.arange(length, dtype=jnp.int32)
    inside = (starts[:, None, :] <= places[None, :, None]).astype(jnp.int32)
    return jnp.sum(inside, axis=-1) - 1


def span_attend(queries, key_rows, value_rows, log_decay, segments):
    batch, length, head_count, key_dim = queries.shape
    value_dim = value_rows.shape[-1]
    spans = length // SPAN
    queries = queries.reshape(batch, spans, SPAN, head_count, key_dim)
    key_rows = key_rows.reshape(batch, spans, SPAN, head_count, key_dim)
    value_rows = value_rows.reshape(batch, spans, SPAN, head_count, value_dim)
    log_decay = log_decay.reshape(batch, spans, SPAN, head_count, key_dim)
    segments = segments.reshape(batch, spans, SPAN)
    cumulative = jnp.cumsum(log_decay, axis=2)
    final_log = cumulative[:, :, -1:]
    q_scaled = queries * jnp.exp(cumulative)
    k_scaled = key_rows * jnp.exp(-cumulative)
    k_to_end = key_rows * jnp.exp(final_log - cumulative)
    places = jnp.arange(SPAN, dtype=jnp.int32)
    causal = places[:, None] >= places[None, :]
    allowed = ((segments[..., :, None] == segments[..., None, :]) & causal).astype(jnp.float32)
    scores = (
        jnp.einsum("bnihk,bnjhk->bnhij", q_scaled, k_scaled, precision=exact_mode)
        * allowed[:, :, None]
    )
    within = jnp.einsum("bnhij,bnjhv->bnihv", scores, value_rows, precision=exact_mode)
    seg_last = segments[:, :, -1]
    tail_mask = (segments == seg_last[..., None]).astype(jnp.float32)
    update = jnp.einsum(
        "bnjhk,bnjhv->bnhkv",
        k_to_end * tail_mask[..., None, None],
        value_rows,
        precision=exact_mode,
    )
    seg_prev = jnp.concatenate([jnp.full((batch, 1), -1, jnp.int32), seg_last[:, :-1]], axis=1)
    carry_on = (seg_last == seg_prev).astype(jnp.float32)
    fade_out = jnp.exp(final_log[:, :, 0])

    def advance(carried, inputs):
        fade_now, keep_now, update_now = inputs
        before = carried
        carried = carried * (fade_now * keep_now[:, None, None])[..., None] + update_now
        return (carried, before)

    start_state = jnp.zeros((batch, head_count, key_dim, value_dim), jnp.float32)
    _, states = lax.scan(
        advance,
        start_state,
        (jnp.moveaxis(fade_out, 1, 0), jnp.moveaxis(carry_on, 1, 0), jnp.moveaxis(update, 1, 0)),
    )
    states = jnp.moveaxis(states, 0, 1)
    reads_old = (segments == seg_prev[..., None]).astype(jnp.float32)
    across = jnp.einsum(
        "bnihk,bnhkv->bnihv", q_scaled * reads_old[..., None, None], states, precision=exact_mode
    )
    return (within + across).reshape(batch, length, head_count, value_dim)


def local_mixer(segments, queries, key_rows, value_rows, gate_rows, decay_pre, gain_head):
    row_count = queries.shape[0]
    head_count = queries.shape[1] // HK
    seq_count = row_count // SEQ_LEN
    log_decay = jax.nn.log_sigmoid(decay_pre) / 16.0
    attended = span_attend(
        (queries * HK ** (-0.5)).reshape(seq_count, SEQ_LEN, head_count, HK),
        key_rows.reshape(seq_count, SEQ_LEN, head_count, HK),
        value_rows.reshape(seq_count, SEQ_LEN, head_count, HV),
        log_decay.reshape(seq_count, SEQ_LEN, head_count, HK),
        segments,
    )
    attended = attended.reshape(row_count, head_count, HV)
    normed = (
        attended
        * lax.rsqrt(jnp.mean(attended * attended, axis=-1, keepdims=True) + head_eps)
        * gain_head
    )
    return normed.reshape(row_count, head_count * HV) * jax.nn.silu(gate_rows)


def per_device(
    tokens_in,
    cotangent,
    doc_lengths,
    mixer_gain,
    w_query,
    w_key,
    w_value,
    w_outgate,
    w_rank_in,
    w_rank_out,
    decay_bias,
    head_gain,
    w_output,
    ffn_gain,
    w_gate,
    w_up,
    w_down,
):
    inputs = tokens_in.astype(jnp.float32)
    inv_one = lax.rsqrt(feature_sum(jnp.sum(inputs * inputs, axis=1)) / D + norm_eps)
    normed_one = inputs * inv_one[:, None]
    gain_one = mixer_gain.astype(jnp.float32)
    first_all = col_tokens((normed_one * gain_one).astype(jnp.bfloat16))
    partials = (
        product(first_all, w_query),
        product(first_all, w_key),
        product(first_all, w_value),
        product(first_all, w_outgate),
        product(first_all, w_rank_in),
    )
    queries, key_rows, value_rows, gate_rows, rank_rows = (
        lax.psum_scatter(partials[0], "row", scatter_dimension=0, tiled=True),
        lax.psum_scatter(partials[1], "row", scatter_dimension=0, tiled=True),
        lax.psum_scatter(partials[2], "row", scatter_dimension=0, tiled=True),
        lax.psum_scatter(partials[3], "row", scatter_dimension=0, tiled=True),
        lax.psum_scatter(partials[4], "row", scatter_dimension=0, tiled=True),
    )
    rank_out = w_rank_out.astype(jnp.float32)
    decay_pre = jnp.dot(rank_rows, rank_out, precision=exact_mode) + decay_bias.astype(jnp.float32)
    segments = segment_ids(doc_lengths, SEQ_LEN)
    mixed, mixer_pull = jax.vjp(
        partial(local_mixer, segments),
        queries,
        key_rows,
        value_rows,
        gate_rows,
        decay_pre,
        head_gain.astype(jnp.float32),
    )
    heads_all = lax.all_gather(mixed.astype(jnp.bfloat16), "row", axis=0, tiled=True)
    residual = inputs + col_parts(product(heads_all, w_output))
    inv_two = lax.rsqrt(feature_sum(jnp.sum(residual * residual, axis=1)) / D + norm_eps)
    normed_two = residual * inv_two[:, None]
    gain_two = ffn_gain.astype(jnp.float32)
    second_all = col_tokens((normed_two * gain_two).astype(jnp.bfloat16))
    gate_pre, up_pre = (
        lax.psum_scatter(product(second_all, w_gate), "row", scatter_dimension=0, tiled=True),
        lax.psum_scatter(product(second_all, w_up), "row", scatter_dimension=0, tiled=True),
    )
    sigmoid_gate = jax.nn.sigmoid(gate_pre)
    silu_gate = gate_pre * sigmoid_gate
    hidden_all = lax.all_gather(
        (silu_gate * up_pre).astype(jnp.bfloat16), "row", axis=0, tiled=True
    )
    output_rows = (residual + col_parts(product(hidden_all, w_down))).astype(jnp.bfloat16)
    grad_out = cotangent.astype(jnp.float32)
    cot_all = col_tokens(cotangent)
    grad_down_w = gram_of(hidden_all, cot_all)
    hidden_grad = lax.psum_scatter(
        times_transpose(cot_all, w_down), "row", scatter_dimension=0, tiled=True
    )
    gate_grad = (
        hidden_grad * up_pre * sigmoid_gate * (1.0 + gate_pre * (1.0 - sigmoid_gate))
    ).astype(jnp.bfloat16)
    up_grad = (hidden_grad * silu_gate).astype(jnp.bfloat16)
    gate_grad_all, up_grad_all = (
        lax.all_gather(gate_grad, "row", axis=0, tiled=True),
        lax.all_gather(up_grad, "row", axis=0, tiled=True),
    )
    grad_gate_w = gram_of(second_all, gate_grad_all)
    grad_up_w = gram_of(second_all, up_grad_all)
    second_grad = col_parts(
        times_transpose(gate_grad_all, w_gate) + times_transpose(up_grad_all, w_up)
    )
    scaled_two = second_grad * gain_two
    gain_two_part = jnp.sum(second_grad * normed_two, axis=0)
    mean_two = feature_sum(jnp.sum(scaled_two * normed_two, axis=1)) / D
    resid_grad = grad_out + inv_two[:, None] * (scaled_two - normed_two * mean_two[:, None])
    resid_all = col_tokens(resid_grad.astype(jnp.bfloat16))
    grad_output_w = gram_of(heads_all, resid_all)
    mixed_grad = lax.psum_scatter(
        times_transpose(resid_all, w_output).astype(jnp.bfloat16),
        "row",
        scatter_dimension=0,
        tiled=True,
    ).astype(jnp.float32)
    query_grad, key_grad, value_grad, outgate_grad, decay_grad, head_gain_part = mixer_pull(
        mixed_grad
    )
    decay_low = decay_grad.astype(jnp.bfloat16)
    sent = (
        query_grad.astype(jnp.bfloat16),
        key_grad.astype(jnp.bfloat16),
        value_grad.astype(jnp.bfloat16),
        outgate_grad.astype(jnp.bfloat16),
        decay_low,
    )
    query_all, key_all, value_all, outgate_all, decay_all = (
        lax.all_gather(sent[0], "row", axis=0, tiled=True),
        lax.all_gather(sent[1], "row", axis=0, tiled=True),
        lax.all_gather(sent[2], "row", axis=0, tiled=True),
        lax.all_gather(sent[3], "row", axis=0, tiled=True),
        lax.all_gather(sent[4], "row", axis=0, tiled=True),
    )
    grad_query_w = gram_of(first_all, query_all)
    grad_key_w = gram_of(first_all, key_all)
    grad_value_w = gram_of(first_all, value_all)
    grad_outgate_w = gram_of(first_all, outgate_all)
    rank_grad = lax.dot_general(
        decay_all.astype(jnp.float32),
        rank_out,
        contract_cols,
        precision=exact_mode,
        preferred_element_type=jnp.float32,
    )
    rank_in_part = lax.dot_general(
        first_all.astype(jnp.float32),
        rank_grad,
        contract_rows,
        precision=exact_mode,
        preferred_element_type=jnp.float32,
    )
    decay_local = decay_low.astype(jnp.float32)
    rank_out_part = lax.dot_general(
        rank_rows,
        decay_local,
        contract_rows,
        precision=exact_mode,
        preferred_element_type=jnp.float32,
    )
    bias_part = jnp.sum(decay_local, axis=0)
    rank_back = lax.dot_general(
        rank_grad,
        w_rank_in.astype(jnp.float32),
        contract_cols,
        precision=exact_mode,
        preferred_element_type=jnp.float32,
    )
    first_grad = col_parts(
        times_transpose(query_all, w_query)
        + times_transpose(key_all, w_key)
        + times_transpose(value_all, w_value)
        + times_transpose(outgate_all, w_outgate)
        + rank_back
    )
    scaled_one = first_grad * gain_one
    gain_one_part = jnp.sum(first_grad * normed_one, axis=0)
    mean_one = feature_sum(jnp.sum(scaled_one * normed_one, axis=1)) / D
    grad_tokens = resid_grad + inv_one[:, None] * (scaled_one - normed_one * mean_one[:, None])
    every_sum = data_sum(
        (
            grad_query_w,
            grad_key_w,
            grad_value_w,
            grad_outgate_w,
            grad_output_w,
            grad_gate_w,
            grad_up_w,
            grad_down_w,
        )
    )
    (
        grad_query_w,
        grad_key_w,
        grad_value_w,
        grad_outgate_w,
        grad_output_w,
        grad_gate_w,
        grad_up_w,
        grad_down_w,
    ) = every_sum
    row_at = lax.axis_index("row")
    col_at = lax.axis_index("col")
    feature_width = mixer_gain.shape[0]
    key_width = decay_bias.shape[0]
    rank_count = w_rank_in.shape[1]
    full_one = lax.dynamic_update_slice(
        jnp.zeros((D,), jnp.float32), gain_one_part, (row_at * feature_width,)
    )
    full_two = lax.dynamic_update_slice(
        jnp.zeros((D,), jnp.float32), gain_two_part, (row_at * feature_width,)
    )
    full_rank_in = lax.dynamic_update_slice(
        jnp.zeros((D, rank_count), jnp.float32), rank_in_part, (row_at * feature_width, 0)
    )
    full_rank_out = lax.dynamic_update_slice(
        jnp.zeros((rank_count, DK), jnp.float32), rank_out_part, (0, col_at * key_width)
    )
    full_bias = lax.dynamic_update_slice(
        jnp.zeros((DK,), jnp.float32), bias_part, (col_at * key_width,)
    )
    sum_one, sum_two, sum_rank_in, sum_rank_out, sum_bias, sum_head = lax.psum(
        (full_one, full_two, full_rank_in, full_rank_out, full_bias, head_gain_part),
        ("dp", "row", "col"),
    )
    grad_mixer_gain = lax.dynamic_slice_in_dim(sum_one, row_at * feature_width, feature_width, 0)
    grad_ffn_gain = lax.dynamic_slice_in_dim(sum_two, row_at * feature_width, feature_width, 0)
    grad_rank_in = lax.dynamic_slice_in_dim(sum_rank_in, row_at * feature_width, feature_width, 0)
    grad_rank_out = lax.dynamic_slice_in_dim(sum_rank_out, col_at * key_width, key_width, 1)
    grad_bias = lax.dynamic_slice_in_dim(sum_bias, col_at * key_width, key_width, 0)
    return (
        output_rows,
        grad_tokens,
        grad_mixer_gain,
        grad_query_w,
        grad_key_w,
        grad_value_w,
        grad_outgate_w,
        grad_rank_in,
        grad_rank_out,
        grad_bias,
        sum_head,
        grad_output_w,
        grad_ffn_gain,
        grad_gate_w,
        grad_up_w,
        grad_down_w,
    )


def solution(mesh):
    in_specs = (
        P(("dp", "col"), "row"),
        P(("dp", "col"), "row"),
        P(("dp", "row"), None),
        P("row"),
        P("row", "col"),
        P("row", "col"),
        P("row", "col"),
        P("row", "col"),
        P("row", None),
        P(None, "col"),
        P("col"),
        P(),
        P("col", "row"),
        P("row"),
        P("row", "col"),
        P("row", "col"),
        P("col", "row"),
    )
    out_specs = (
        P(("dp", "col"), "row"),
        P(("dp", "col"), "row"),
        P("row"),
        P("row", "col"),
        P("row", "col"),
        P("row", "col"),
        P("row", "col"),
        P("row", None),
        P(None, "col"),
        P("col"),
        P(),
        P("col", "row"),
        P("row"),
        P("row", "col"),
        P("row", "col"),
        P("col", "row"),
    )
    return jax.shard_map(
        per_device, mesh=mesh, in_specs=in_specs, out_specs=out_specs, check_vma=False
    )
```

profile of v0, /device:TPU:0, one launch (start us, length us, event | category | flops | bytes accessed | tf_op | source)
XLA Modules:
  0.0 2682.3 jit_solution(10545545383116421357)
XLA Ops:
  21.3 81.1 %all-gather.14.cloned.1.call-done = bf16[8192,256]{1,0:T(8,128)(2,1)} async-done(((bf16[2048,256]{1,0:T(8,128)(2,1)}), bf16[8192,256]{1,0:T(8,128)(2,1)}) %all-gather.14.cloned.1.call-update) | async-done | bytes 4194320 | tf_op jit(solution)/shard_map/all_gather | solution.py:37
  144.3 29.8 %reduce-scatter.16.cloned.1.call-done = f32[2048,128]{1,0:T(8,128)} async-done(((f32[8192,128]{1,0:T(8,128)}), f32[2048,128]{1,0:T(8,128)}) %reduce-scatter.16.cloned.1.call-update) | async-done | bytes 1048592 | tf_op jit(solution)/shard_map/reduce_scatter | solution.py:171
  175.4 45.7 %reduce-scatter.20.cloned.1.call-done = f32[2048,128]{1,0:T(8,128)} async-done(((f32[8192,128]{1,0:T(8,128)}), f32[2048,128]{1,0:T(8,128)}) %reduce-scatter.20.cloned.1.call-update) | async-done | bytes 1048592 | tf_op jit(solution)/shard_map/reduce_scatter | solution.py:172
  226.3 68.6 %reduce-scatter.14.cloned.1.call-done = f32[2048,256]{1,0:T(8,128)} async-done(((f32[8192,256]{1,0:T(8,128)}), f32[2048,256]{1,0:T(8,128)}) %reduce-scatter.14.cloned.1.call-update) | async-done | bytes 2097168 | tf_op jit(solution)/shard_map/reduce_scatter | solution.py:173
  310.3 196.0 %while.36 = (s32[]{:T(128)}, f32[1,1,128,256]{3,2,1,0:T(8,128)S(1)}, f32[32,1,1,128,256]{4,3,2,1,0:T(8,128)}, f32[32,1,1,1]{0,3,2,1:T(1,128)S(1)}, f32[32,1,1,12...) while((s32[]{:T(128)}, ...), condition=%wide.region_10.11_spmd.clone, body=%wide.region_9.10_spmd.clone.sunk | while | flops 131331 | bytes 659604 | solution.py:105
  520.2 34.5 %all-gather.16.cloned.1.call-done = bf16[8192,256]{1,0:T(8,128)(2,1)} async-done(((bf16[2048,256]{1,0:T(8,128)(2,1)}), bf16[8192,256]{1,0:T(8,128)(2,1)}) %all-gather.16.cloned.1.call-update) | async-done | bytes 4194320 | tf_op jit(solution)/shard_map/all_gather | solution.py:189
  562.8 143.4 %reduce-scatter.24.cloned.1.call-done = f32[2048,256]{1,0:T(8,128)} async-done(((f32[8192,256]{1,0:T(8,128)}), f32[2048,256]{1,0:T(8,128)}) %reduce-scatter.24.cloned.1.call-update) | async-done | bytes 2097168 | tf_op jit(solution)/shard_map/reduce_scatter | solution.py:41
  719.6 69.6 %all-gather.22.cloned.1.call-done = bf16[8192,256]{1,0:T(8,128)(2,1)} async-done(((bf16[2048,256]{1,0:T(8,128)(2,1)}), bf16[8192,256]{1,0:T(8,128)(2,1)}) %all-gather.22.cloned.1.call-update) | async-done | bytes 4194320 | tf_op jit(solution)/shard_map/all_gather | solution.py:37
  789.2 14.1 fusion.104
  803.3 66.5 %all-gather.18.cloned.1.call-done = bf16[8192,256]{1,0:T(8,128)(2,1)} async-done(((bf16[2048,256]{1,0:T(8,128)(2,1)}), bf16[8192,256]{1,0:T(8,128)(2,1)}) %all-gather.18.cloned.1.call-update) | async-done | bytes 4194320 | tf_op jit(solution)/shard_map/all_gather | solution.py:37
  869.9 16.6 fusion.101
  886.6 16.8 fusion.102
  903.5 130.5 %reduce-scatter.32.cloned.1.call-done = f32[2048,704]{0,1:T(8,128)} async-done(((f32[8192,704]{0,1:T(8,128)}), f32[2048,704]{0,1:T(8,128)}) %reduce-scatter.32.cloned.1.call-update) | async-done | bytes 5767184 | tf_op jit(solution)/shard_map/reduce_scatter | solution.py:208
  1034.0 165.5 %reduce-scatter.26.cloned.1.call-done = f32[2048,704]{0,1:T(8,128)} async-done(((f32[8192,704]{0,1:T(8,128)}), f32[2048,704]{0,1:T(8,128)}) %reduce-scatter.26.cloned.1.call-update) | async-done | bytes 5767184 | tf_op jit(solution)/shard_map/reduce_scatter | solution.py:196
  1199.5 165.6 %reduce-scatter.28.cloned.1.call-done = f32[2048,704]{0,1:T(8,128)} async-done(((f32[8192,704]{0,1:T(8,128)}), f32[2048,704]{0,1:T(8,128)}) %reduce-scatter.28.cloned.1.call-update) | async-done | bytes 5767184 | tf_op jit(solution)/shard_map/reduce_scatter | solution.py:197
  1376.9 75.3 %all-gather.24.cloned.1.call-done = bf16[8192,704]{0,1:T(8,128)(2,1)} async-done(((bf16[2048,704]{0,1:T(8,128)(2,1)}), bf16[8192,704]{0,1:T(8,128)(2,1)}) %all-gather.24.cloned.1.call-update) | async-done | bytes 11534352 | tf_op jit(solution)/shard_map/all_gather | solution.py:216
  1452.1 12.1 fusion.105
  1464.3 65.4 %all-gather.26.cloned.1.call-done = bf16[8192,704]{0,1:T(8,128)(2,1)} async-done(((bf16[2048,704]{0,1:T(8,128)(2,1)}), bf16[8192,704]{0,1:T(8,128)(2,1)}) %all-gather.26.cloned.1.call-update) | async-done | bytes 11534352 | tf_op jit(solution)/shard_map/all_gather | solution.py:217
  1529.7 13.6 convolution_add_fusion.4
  1543.4 144.7 %reduce-scatter.34.cloned.1.call-done = f32[2048,256]{1,0:T(8,128)} async-done(((f32[8192,256]{1,0:T(8,128)}), f32[2048,256]{1,0:T(8,128)}) %reduce-scatter.34.cloned.1.call-update) | async-done | bytes 2097168 | tf_op jit(solution)/shard_map/reduce_scatter | solution.py:41
  1700.6 81.2 %all-gather.28.cloned.1.call-done = bf16[8192,256]{1,0:T(8,128)(2,1)} async-done(((bf16[2048,256]{1,0:T(8,128)(2,1)}), bf16[8192,256]{1,0:T(8,128)(2,1)}) %all-gather.28.cloned.1.call-update) | async-done | bytes 4194320 | tf_op jit(solution)/shard_map/all_gather | solution.py:37
  1788.1 42.4 %reduce-scatter.36.cloned.1.call-done = bf16[2048,256]{1,0:T(8,128)(2,1)} async-done(((bf16[8192,256]{1,0:T(8,128)(2,1)}), bf16[2048,256]{1,0:T(8,128)(2,1)}) %reduce-scatter.36.cloned.1.call-update) | async-done | bytes 1048592 | tf_op jit(solution)/shard_map/reduce_scatter | solution.py:230
  1849.0 171.0 %while.37 = (s32[]{:T(128)}, f32[1,1,128,256]{3,2,1,0:T(8,128)S(1)}, f32[32,1,1,128]{3,2,1,0:T(1,128)S(1)}, f32[32,1,1,128,256]{4,3,2,1,0:T(8,128)}, f32[32,1,1,...) while((s32[]{:T(128)}, ...), condition=%wide.region_27.28_spmd.clone, body=%wide.region_25.27_spmd.clone.sunk | while | flops 196612 | bytes 1313960 | solution.py:105
  2104.3 15.3 all-gather.32.cloned.1.call-done
  2132.9 23.4 all-gather.34.cloned.1.call-done
  2161.7 31.1 %all-gather.36.cloned.1.call-done = bf16[8192,256]{1,0:T(8,128)(2,1)} async-done(((bf16[2048,256]{1,0:T(8,128)(2,1)}), bf16[8192,256]{1,0:T(8,128)(2,1)}) %all-gather.36.cloned.1.call-update) | async-done | bytes 4194320 | tf_op jit(solution)/shard_map/all_gather | solution.py:251
  2212.4 11.1 fusion.103
  2225.0 92.7 %all-reduce.6.cloned.1.call-done = f32[1024,16]{0,1:T(8,128)} async-done(((f32[1024,16]{0,1:T(8,128)}), f32[1024,16]{0,1:T(8,128)}) %all-reduce.6.cloned.1.call-update) | async-done | bytes 65552 | tf_op jit(solution)/shard_map/psum | solution.py:341
  2319.0 56.0 %all-reduce.8.cloned.1.call-done = (bf16[256,128]{1,0:T(8,128)(2,1)}, bf16[256,128]{1,0:T(8,128)(2,1)}, bf16[256,256]{1,0:T(8,128)(2,1)}, bf16[256,256]{1,0:T(8,...) async-done(((bf16[256,128]{1,0:T(8,128)(2,1)}, bf16[256,128]{1,0:T(8,128)(2,1)}, ...) | async-done | bytes 1605648 | tf_op jit(solution)/shard_map/psum | solution.py:46
  2387.0 134.9 %reduce-scatter.38.cloned.1.call-done = f32[2048,256]{1,0:T(8,128)} async-done(((f32[8192,256]{1,0:T(8,128)}), f32[2048,256]{1,0:T(8,128)}) %reduce-scatter.38.cloned.1.call-update) | async-done | bytes 2097168 | tf_op jit(solution)/shard_map/reduce_scatter | solution.py:41
  2524.6 46.0 %all-reduce.1 = (f32[1024]{0:T(1024)S(1)}, f32[16,512]{1,0:T(8,128)S(1)}, f32[512]{0:T(512)S(1)}, f32[256]{0:T(256)}, f32[1024]{0:T(1024)S(1)}) all-reduce(f32[1024]{0:T(1024)S(1)} %dynamic_update_slice.46, f32[16,512]{1,0:T(8,128)S(1)} %convolution_dynamic-update-slice_fusion.1, ...), channel_id=1, replica_groups=mesh['dp'=2,'row'=4,'col'=4] {'dp','row','col'}, use_global_device_ids=true, to_apply=%region_34.35 | all-reduce | flops 11008 | bytes 88064 | tf_op jit(solution)/shard_map/psum | solution.py:341
  2579.2 91.2 %reduce-scatter.30.cloned.1.call-done = f32[2048,256]{1,0:T(8,128)} async-done(((f32[8192,256]{1,0:T(8,128)}), f32[2048,256]{1,0:T(8,128)}) %reduce-scatter.30.cloned.1.call-update) | async-done | bytes 2097168 | tf_op jit(solution)/shard_map/reduce_scatter | solution.py:41
  (737 shorter events, 680.6 us)
Async XLA Ops:
  7.2 862.7 %copy-start = (bf16[256,704]{0,1:T(8,128)(2,1)S(1)}, bf16[256,704]{0,1:T(8,128)(2,1)}, u32[]{:S(2)}) copy-start(bf16[256,704]{0,1:T(8,128)(2,1)} %param.35) | copy-start | bytes 1081348
  7.2 95.2 %all-gather.14.cloned.1.call-start = ((), (), s32[]{:S(2)}) async-start(), calls=%async_computation.13 | async-start | bytes 5242880 | tf_op jit(solution)/shard_map/all_gather | solution.py:37
  21.2 116.6 %reduce-scatter.18.cloned.1.call-start = ((), (), s32[]{:S(2)}) async-start(), calls=%async_computation.16 | async-start | bytes 655360 | tf_op jit(solution)/shard_map/reduce_scatter | solution.py:175
  106.6 67.4 %reduce-scatter.16.cloned.1.call-start = ((), (), s32[]{:S(2)}) async-start(), calls=%async_computation.15 | async-start | bytes 5242880 | tf_op jit(solution)/shard_map/reduce_scatter | solution.py:171
  112.2 108.9 %reduce-scatter.20.cloned.1.call-start = ((), (), s32[]{:S(2)}) async-start(), calls=%async_computation.17 | async-start | bytes 5242880 | tf_op jit(solution)/shard_map/reduce_scatter | solution.py:172
  118.5 176.5 %reduce-scatter.14.cloned.1.call-start = ((), (), s32[]{:S(2)}) async-start(), calls=%async_computation.14 | async-start | bytes 10485760 | tf_op jit(solution)/shard_map/reduce_scatter | solution.py:173
  126.2 390.4 %reduce-scatter.22.cloned.1.call-start = ((), (), s32[]{:S(2)}) async-start(), calls=%async_computation.18 | async-start | bytes 10485760 | tf_op jit(solution)/shard_map/reduce_scatter | solution.py:174
  137.5 417.2 %all-gather.16.cloned.1.call-start = ((), (), s32[]{:S(2)}) async-start(), calls=%async_computation.19 | async-start | bytes 5242880 | tf_op jit(solution)/shard_map/all_gather | solution.py:189
  520.1 186.1 %reduce-scatter.24.cloned.1.call-start = ((), (), s32[]{:S(2)}) async-start(), calls=%async_computation.20 | async-start | bytes 10485760 | tf_op jit(solution)/shard_map/reduce_scatter | solution.py:41
  561.5 227.7 %all-gather.22.cloned.1.call-start = ((), (), s32[]{:S(2)}) async-start(), calls=%async_computation.26 | async-start | bytes 5242880 | tf_op jit(solution)/shard_map/all_gather | solution.py:37
  562.2 307.7 %all-gather.18.cloned.1.call-start = ((), (), s32[]{:S(2)}) async-start(), calls=%async_computation.21 | async-start | bytes 5242880 | tf_op jit(solution)/shard_map/all_gather | solution.py:37
  709.0 988.4 %copy-start.2 = (f32[2048,256]{1,0:T(8,128)}, f32[2048,256]{1,0:T(8,128)S(1)}, u32[]{:S(2)}) copy-start(f32[2048,256]{1,0:T(8,128)S(1)} %get-tuple-element.398) | copy-start | bytes 6291460
  719.3 314.6 %reduce-scatter.32.cloned.1.call-start = ((), (), s32[]{:S(2)}) async-start(), calls=%async_computation.27 | async-start | bytes 28835840 | tf_op jit(solution)/shard_map/reduce_scatter | solution.py:208
  803.3 396.2 %reduce-scatter.26.cloned.1.call-start = ((), (), s32[]{:S(2)}) async-start(), calls=%async_computation.22 | async-start | bytes 28835840 | tf_op jit(solution)/shard_map/reduce_scatter | solution.py:196
  886.5 478.6 %reduce-scatter.28.cloned.1.call-start = ((), (), s32[]{:S(2)}) async-start(), calls=%async_computation.23 | async-start | bytes 28835840 | tf_op jit(solution)/shard_map/reduce_scatter | solution.py:197
  903.4 548.7 %all-gather.24.cloned.1.call-start = ((), (), s32[]{:S(2)}) async-start(), calls=%async_computation.28 | async-start | bytes 14417920 | tf_op jit(solution)/shard_map/all_gather | solution.py:216
  1375.8 153.9 %all-gather.26.cloned.1.call-start = ((), (), s32[]{:S(2)}) async-start(), calls=%async_computation.29 | async-start | bytes 14417920 | tf_op jit(solution)/shard_map/all_gather | solution.py:217
  1376.4 311.7 %reduce-scatter.34.cloned.1.call-start = ((), (), s32[]{:S(2)}) async-start(), calls=%async_computation.30 | async-start | bytes 10485760 | tf_op jit(solution)/shard_map/reduce_scatter | solution.py:41
  1543.4 238.4 %all-gather.28.cloned.1.call-start = ((), (), s32[]{:S(2)}) async-start(), calls=%async_computation.31 | async-start | bytes 5242880 | tf_op jit(solution)/shard_map/all_gather | solution.py:37
  1700.5 130.0 %reduce-scatter.36.cloned.1.call-start = ((), (), s32[]{:S(2)}) async-start(), calls=%async_computation.32 | async-start | bytes 5242880 | tf_op jit(solution)/shard_map/reduce_scatter | solution.py:230
  1787.3 286.9 %all-gather.20.cloned.1.call-start = ((), (), s32[]{:S(2)}) async-start(), calls=%async_computation.24 | async-start | bytes 14417920 | tf_op jit(solution)/shard_map/all_gather | solution.py:201
  1788.0 298.0 %all-gather.38.cloned.1.call-start = ((), (), s32[]{:S(2)}) async-start(), calls=%async_computation.37 | async-start | bytes 2621440 | tf_op jit(solution)/shard_map/all_gather | solution.py:252
  2047.4 47.5 %all-gather.30.cloned.1.call-start = ((), (), s32[]{:S(2)}) async-start(), calls=%async_computation.33 | async-start | bytes 2621440 | tf_op jit(solution)/shard_map/all_gather | solution.py:248
  2048.2 71.5 %all-gather.32.cloned.1.call-start = ((), (), s32[]{:S(2)}) async-start(), calls=%async_computation.34 | async-start | bytes 2621440 | tf_op jit(solution)/shard_map/all_gather | solution.py:249
  2048.9 107.4 %all-gather.34.cloned.1.call-start = ((), (), s32[]{:S(2)}) async-start(), calls=%async_computation.35 | async-start | bytes 5242880 | tf_op jit(solution)/shard_map/all_gather | solution.py:250
  2056.7 136.0 %all-gather.36.cloned.1.call-start = ((), (), s32[]{:S(2)}) async-start(), calls=%async_computation.36 | async-start | bytes 5242880 | tf_op jit(solution)/shard_map/all_gather | solution.py:251
  2057.3 260.4 %all-reduce.6.cloned.1.call-start = ((), (), s32[]{:S(2)}) async-start(), calls=%async_computation.39 | async-start | bytes 131072 | tf_op jit(solution)/shard_map/psum | solution.py:341
  2092.9 282.2 %all-reduce.8.cloned.1.call-start = ((), (), s32[]{:S(2)}) async-start(), calls=%async_computation.40 | async-start | bytes 3211264 | tf_op jit(solution)/shard_map/psum | solution.py:46
  2198.2 323.7 %reduce-scatter.38.cloned.1.call-start = ((), (), s32[]{:S(2)}) async-start(), calls=%async_computation.38 | async-start | bytes 10485760 | tf_op jit(solution)/shard_map/reduce_scatter | solution.py:41
  2211.5 459.0 %reduce-scatter.30.cloned.1.call-start = ((), (), s32[]{:S(2)}) async-start(), calls=%async_computation.25 | async-start | bytes 10485760 | tf_op jit(solution)/shard_map/reduce_scatter | solution.py:41
  2224.9 445.5 %copy-start.3 = (f32[2048,256]{1,0:T(8,128)S(1)}, f32[2048,256]{1,0:T(8,128)}, u32[]{:S(2)}) copy-start(f32[2048,256]{1,0:T(8,128)} %copy-done.2) | copy-start | bytes 6291460
  2224.9 445.5 %copy-start.44 = (f32[2048]{0:T(1024)S(1)}, f32[2048]{0:T(1024)}, u32[]{:S(2)}) copy-start(f32[2048]{0:T(1024)} %copy-done.42) | copy-start | bytes 24580
  (70 other events, 3493.3 us)
Sparse Core Ops, SparseCore 0:
  21.4 81.0 all-gather.13
  106.8 20.1 reduce-scatter.17
  129.4 44.5 reduce-scatter.15
  176.5 44.5 reduce-scatter.19
  223.5 71.3 reduce-scatter.13
  297.4 71.3 reduce-scatter.21
  520.2 34.4 all-gather.15
  561.6 144.6 reduce-scatter.23
  707.8 81.3 all-gather.21
  790.6 79.2 all-gather.17
  872.5 161.4 reduce-scatter.31
  1036.4 162.9 reduce-scatter.25
  1202.1 162.9 reduce-scatter.27
  1376.0 76.1 all-gather.23
  1453.5 76.1 all-gather.25
  1543.5 144.6 reduce-scatter.33
  1700.6 81.0 all-gather.27
  1787.4 43.0 reduce-scatter.35
  1832.0 76.1 all-gather.19
  2047.5 22.5 all-gather.37
  2072.3 22.5 all-gather.29
  2097.0 22.5 all-gather.31
  2121.8 34.4 all-gather.33
  2158.3 34.4 all-gather.35
  2198.3 119.3 all-reduce.5
  2321.4 53.5 all-reduce.7
  2377.2 144.6 reduce-scatter.37
  2524.2 146.1 reduce-scatter.29
where the time goes:
time: 2690 us; the launch traced here: 2680 us
  waiting for transfers between devices  1860 us (69%)
  other arithmetic  296 us (11%)
  matrix products  274 us (10%)
  local copies, waits for them, and re-layouts  158 us (6%)
  blocking collectives  74 us (3%)
    reduce_scatter x4, waiting for transfers between devices, col_parts(): return lax.psum_scatter(partial_sum, 'col', scatter_dimension=0, tiled=True)  514 us
    all_gather x4, waiting for transfers between devices, col_tokens(): return lax.all_gather(block, 'col', axis=0, tiled=True)  298 us
    reduce_scatter x1, waiting for transfers between devices, per_device(): lax.psum_scatter(product(second_all, w_up), 'row', scatter_dimension=0, t...  166 us
    reduce_scatter x1, waiting for transfers between devices, per_device(): lax.psum_scatter(product(second_all, w_gate), 'row', scatter_dimension=0,...  165 us
    reduce_scatter x1, waiting for transfers between devices, per_device(): lax.psum_scatter(times_transpose(cot_all, w_down), 'row', scatter_dimensi...  130 us
    dynamic_update_slice x128, other arithmetic, span_attend(): lax.scan(advance, start_state, (jnp.moveaxis(fade_out, 1, 0), jnp.moveaxi...  121 us
    psum x1, waiting for transfers between devices, per_device(): lax.psum((full_one, full_two, full_rank_in, full_rank_out, full_bias, hea...  92.7 us
    dynamic_slice x128, local copies, waits for them, and re-layouts, span_attend(): lax.scan(advance, start_state, (jnp.moveaxis(fade_out, 1, 0), jnp.moveaxi...  91 us
  transfers between devices with their start and end apart: 28, of which 24 were waited for; matrix products, arithmetic and copies ran while one was open for 25% of the time, Pallas kernels for 0%

commit v1 on v0

--- a/solution.py
+++ b/solution.py
@@ -3,6 +3,7 @@
 import jax.numpy as jnp
 from jax import lax
 from jax.sharding import PartitionSpec as P
+from jax.lax import all_gather
 
 D = 1024
 DK = 512
@@ -42,8 +43,9 @@
 
 
 def data_sum(group):
+    _push_views = lambda x_part: all_gather(x_part, "dp").sum(axis=0)
     return (
-        lax.psum(group[0].astype(jnp.bfloat16), "dp").astype(jnp.float32),
+        _push_views(group[0].astype(jnp.bfloat16)).astype(jnp.float32),
         lax.psum(group[1].astype(jnp.bfloat16), "dp").astype(jnp.float32),
         lax.psum(group[2].astype(jnp.bfloat16), "dp").astype(jnp.float32),
         lax.psum(group[3].astype(jnp.bfloat16), "dp").astype(jnp.float32),

time: 2690 us -> 2690 us (level)
  transfers between devices with their start and end apart: 28 -> 28, of which waited for: 24 -> 24; matrix products, arithmetic and copies ran while one was open for 25% -> 24% of each run, Pallas kernels for 0% -> 0%
where the time goes in v1:
time: 2690 us; the launch traced here: 2680 us
  waiting for transfers between devices  1860 us (69%)
  other arithmetic  296 us (11%)
  matrix products  267 us (10%)
  local copies, waits for them, and re-layouts  159 us (6%)
  blocking collectives  79.2 us (3%)
    reduce_scatter x4, waiting for transfers between devices, col_parts(): return lax.psum_scatter(partial_sum, 'col', scatter_dimension=0, tiled=True)  515 us
    all_gather x4, waiting for transfers between devices, col_tokens(): return lax.all_gather(block, 'col', axis=0, tiled=True)  298 us
    reduce_scatter x1, waiting for transfers between devices, per_device(): lax.psum_scatter(product(second_all, w_up), 'row', scatter_dimension=0, t...  166 us
    reduce_scatter x1, waiting for transfers between devices, per_device(): lax.psum_scatter(product(second_all, w_gate), 'row', scatter_dimension=0,...  165 us
    reduce_scatter x1, waiting for transfers between devices, per_device(): lax.psum_scatter(times_transpose(cot_all, w_down), 'row', scatter_dimensi...  130 us
    dynamic_update_slice x128, other arithmetic, span_attend(): lax.scan(advance, start_state, (jnp.moveaxis(fade_out, 1, 0), jnp.moveaxi...  121 us
    dynamic_slice x128, local copies, waits for them, and re-layouts, span_attend(): lax.scan(advance, start_state, (jnp.moveaxis(fade_out, 1, 0), jnp.moveaxi...  91 us
    psum x1, waiting for transfers between devices, per_device(): lax.psum((full_one, full_two, full_rank_in, full_rank_out, full_bias, hea...  82.9 us
  transfers between devices with their start and end apart: 28, of which 24 were waited for; matrix products, arithmetic and copies ran while one was open for 24% of the time, Pallas kernels for 0%

profile of v1, /device:TPU:0, one launch (start us, length us, event | category | flops | bytes accessed | tf_op | source)
XLA Modules:
  0.0 2680.9 jit_solution(12215957015285519546)
XLA Ops:
  21.3 81.1 %all-gather.15.cloned.1.call-done = bf16[8192,256]{1,0:T(8,128)(2,1)} async-done(((bf16[2048,256]{1,0:T(8,128)(2,1)}), bf16[8192,256]{1,0:T(8,128)(2,1)}) %all-gather.15.cloned.1.call-update) | async-done | bytes 4194320 | tf_op jit(solution)/shard_map/all_gather | solution.py:38
  144.3 29.7 %reduce-scatter.16.cloned.1.call-done = f32[2048,128]{1,0:T(8,128)} async-done(((f32[8192,128]{1,0:T(8,128)}), f32[2048,128]{1,0:T(8,128)}) %reduce-scatter.16.cloned.1.call-update) | async-done | bytes 1048592 | tf_op jit(solution)/shard_map/reduce_scatter | solution.py:173
  175.4 45.7 %reduce-scatter.20.cloned.1.call-done = f32[2048,128]{1,0:T(8,128)} async-done(((f32[8192,128]{1,0:T(8,128)}), f32[2048,128]{1,0:T(8,128)}) %reduce-scatter.20.cloned.1.call-update) | async-done | bytes 1048592 | tf_op jit(solution)/shard_map/reduce_scatter | solution.py:174
  226.3 68.6 %reduce-scatter.14.cloned.1.call-done = f32[2048,256]{1,0:T(8,128)} async-done(((f32[8192,256]{1,0:T(8,128)}), f32[2048,256]{1,0:T(8,128)}) %reduce-scatter.14.cloned.1.call-update) | async-done | bytes 2097168 | tf_op jit(solution)/shard_map/reduce_scatter | solution.py:175
  310.3 195.9 %while.36 = (s32[]{:T(128)}, f32[1,1,128,256]{3,2,1,0:T(8,128)S(1)}, f32[32,1,1,128,256]{4,3,2,1,0:T(8,128)}, f32[32,1,1,1]{0,3,2,1:T(1,128)S(1)}, f32[32,1,1,12...) while((s32[]{:T(128)}, ...), condition=%wide.region_10.11_spmd.clone, body=%wide.region_9.10_spmd.clone.sunk | while | flops 131331 | bytes 659604 | solution.py:107
  520.1 34.5 %all-gather.17.cloned.1.call-done = bf16[8192,256]{1,0:T(8,128)(2,1)} async-done(((bf16[2048,256]{1,0:T(8,128)(2,1)}), bf16[8192,256]{1,0:T(8,128)(2,1)}) %all-gather.17.cloned.1.call-update) | async-done | bytes 4194320 | tf_op jit(solution)/shard_map/all_gather | solution.py:191
  562.8 143.4 %reduce-scatter.24.cloned.1.call-done = f32[2048,256]{1,0:T(8,128)} async-done(((f32[8192,256]{1,0:T(8,128)}), f32[2048,256]{1,0:T(8,128)}) %reduce-scatter.24.cloned.1.call-update) | async-done | bytes 2097168 | tf_op jit(solution)/shard_map/reduce_scatter | solution.py:42
  719.5 69.6 %all-gather.23.cloned.1.call-done = bf16[8192,256]{1,0:T(8,128)(2,1)} async-done(((bf16[2048,256]{1,0:T(8,128)(2,1)}), bf16[8192,256]{1,0:T(8,128)(2,1)}) %all-gather.23.cloned.1.call-update) | async-done | bytes 4194320 | tf_op jit(solution)/shard_map/all_gather | solution.py:38
  789.1 14.1 fusion.104
  803.3 66.5 %all-gather.19.cloned.1.call-done = bf16[8192,256]{1,0:T(8,128)(2,1)} async-done(((bf16[2048,256]{1,0:T(8,128)(2,1)}), bf16[8192,256]{1,0:T(8,128)(2,1)}) %all-gather.19.cloned.1.call-update) | async-done | bytes 4194320 | tf_op jit(solution)/shard_map/all_gather | solution.py:38
  869.8 16.6 fusion.101
  886.5 16.9 fusion.102
  903.4 130.5 %reduce-scatter.32.cloned.1.call-done = f32[2048,704]{0,1:T(8,128)} async-done(((f32[8192,704]{0,1:T(8,128)}), f32[2048,704]{0,1:T(8,128)}) %reduce-scatter.32.cloned.1.call-update) | async-done | bytes 5767184 | tf_op jit(solution)/shard_map/reduce_scatter | solution.py:210
  1033.9 165.5 %reduce-scatter.26.cloned.1.call-done = f32[2048,704]{0,1:T(8,128)} async-done(((f32[8192,704]{0,1:T(8,128)}), f32[2048,704]{0,1:T(8,128)}) %reduce-scatter.26.cloned.1.call-update) | async-done | bytes 5767184 | tf_op jit(solution)/shard_map/reduce_scatter | solution.py:198
  1199.4 165.6 %reduce-scatter.28.cloned.1.call-done = f32[2048,704]{0,1:T(8,128)} async-done(((f32[8192,704]{0,1:T(8,128)}), f32[2048,704]{0,1:T(8,128)}) %reduce-scatter.28.cloned.1.call-update) | async-done | bytes 5767184 | tf_op jit(solution)/shard_map/reduce_scatter | solution.py:199
  1376.8 75.3 %all-gather.25.cloned.1.call-done = bf16[8192,704]{0,1:T(8,128)(2,1)} async-done(((bf16[2048,704]{0,1:T(8,128)(2,1)}), bf16[8192,704]{0,1:T(8,128)(2,1)}) %all-gather.25.cloned.1.call-update) | async-done | bytes 11534352 | tf_op jit(solution)/shard_map/all_gather | solution.py:218
  1452.1 12.1 fusion.105
  1464.2 65.4 %all-gather.27.cloned.1.call-done = bf16[8192,704]{0,1:T(8,128)(2,1)} async-done(((bf16[2048,704]{0,1:T(8,128)(2,1)}), bf16[8192,704]{0,1:T(8,128)(2,1)}) %all-gather.27.cloned.1.call-update) | async-done | bytes 11534352 | tf_op jit(solution)/shard_map/all_gather | solution.py:219
  1529.6 13.6 convolution_add_fusion.4
  1543.4 144.7 %reduce-scatter.34.cloned.1.call-done = f32[2048,256]{1,0:T(8,128)} async-done(((f32[8192,256]{1,0:T(8,128)}), f32[2048,256]{1,0:T(8,128)}) %reduce-scatter.34.cloned.1.call-update) | async-done | bytes 2097168 | tf_op jit(solution)/shard_map/reduce_scatter | solution.py:42
  1700.5 81.2 %all-gather.29.cloned.1.call-done = bf16[8192,256]{1,0:T(8,128)(2,1)} async-done(((bf16[2048,256]{1,0:T(8,128)(2,1)}), bf16[8192,256]{1,0:T(8,128)(2,1)}) %all-gather.29.cloned.1.call-update) | async-done | bytes 4194320 | tf_op jit(solution)/shard_map/all_gather | solution.py:38
  1788.0 42.4 %reduce-scatter.36.cloned.1.call-done = bf16[2048,256]{1,0:T(8,128)(2,1)} async-done(((bf16[8192,256]{1,0:T(8,128)(2,1)}), bf16[2048,256]{1,0:T(8,128)(2,1)}) %reduce-scatter.36.cloned.1.call-update) | async-done | bytes 1048592 | tf_op jit(solution)/shard_map/reduce_scatter | solution.py:232
  1849.0 171.0 %while.37 = (s32[]{:T(128)}, f32[1,1,128,256]{3,2,1,0:T(8,128)S(1)}, f32[32,1,1,128]{3,2,1,0:T(1,128)S(1)}, f32[32,1,1,128,256]{4,3,2,1,0:T(8,128)}, f32[32,1,1,...) while((s32[]{:T(128)}, ...), condition=%wide.region_27.28_spmd.clone, body=%wide.region_25.27_spmd.clone.sunk | while | flops 196612 | bytes 1313960 | solution.py:107
  2099.7 19.9 all-gather.31.cloned.1.call-done
  2127.0 29.3 %all-gather.35.cloned.1.call-done = bf16[8192,256]{1,0:T(8,128)(2,1)} async-done(((bf16[2048,256]{1,0:T(8,128)(2,1)}), bf16[8192,256]{1,0:T(8,128)(2,1)}) %all-gather.35.cloned.1.call-update) | async-done | bytes 4194320 | tf_op jit(solution)/shard_map/all_gather | solution.py:252
  2161.7 31.1 %all-gather.37.cloned.1.call-done = bf16[8192,256]{1,0:T(8,128)(2,1)} async-done(((bf16[2048,256]{1,0:T(8,128)(2,1)}), bf16[8192,256]{1,0:T(8,128)(2,1)}) %all-gather.37.cloned.1.call-update) | async-done | bytes 4194320 | tf_op jit(solution)/shard_map/all_gather | solution.py:253
  2212.4 11.1 fusion.103
  2234.9 82.9 %all-reduce.6.cloned.1.call-done = f32[1024,16]{0,1:T(8,128)} async-done(((f32[1024,16]{0,1:T(8,128)}), f32[1024,16]{0,1:T(8,128)}) %all-reduce.6.cloned.1.call-update) | async-done | bytes 65552 | tf_op jit(solution)/shard_map/psum | solution.py:343
  2319.0 54.6 %all-reduce.8.cloned.1.call-done = (bf16[256,128]{1,0:T(8,128)(2,1)}, bf16[256,256]{1,0:T(8,128)(2,1)}, bf16[256,256]{1,0:T(8,128)(2,1)}, bf16[256,256]{1,0:T(8,...) async-done(((bf16[256,128]{1,0:T(8,128)(2,1)}, bf16[256,256]{1,0:T(8,128)(2,1)}, bf16[256,256]{1,0:T(8,128)(2,1)}, ...) | async-done | bytes 1540112 | tf_op jit(solution)/shard_map/psum | solution.py:49
  2384.9 135.5 %reduce-scatter.38.cloned.1.call-done = f32[2048,256]{1,0:T(8,128)} async-done(((f32[8192,256]{1,0:T(8,128)}), f32[2048,256]{1,0:T(8,128)}) %reduce-scatter.38.cloned.1.call-update) | async-done | bytes 2097168 | tf_op jit(solution)/shard_map/reduce_scatter | solution.py:42
  2523.2 46.0 %all-reduce.1 = (f32[1024]{0:T(1024)S(1)}, f32[16,512]{1,0:T(8,128)S(1)}, f32[512]{0:T(512)S(1)}, f32[256]{0:T(256)}, f32[1024]{0:T(1024)S(1)}) all-reduce(f32[1024]{0:T(1024)S(1)} %dynamic_update_slice.46, f32[16,512]{1,0:T(8,128)S(1)} %convolution_dynamic-update-slice_fusion.1, ...), channel_id=1, replica_groups=mesh['dp'=2,'row'=4,'col'=4] {'dp','row','col'}, use_global_device_ids=true, to_apply=%region_34.35 | all-reduce | flops 11008 | bytes 88064 | tf_op jit(solution)/shard_map/psum | solution.py:343
  2577.8 91.2 %reduce-scatter.30.cloned.1.call-done = f32[2048,256]{1,0:T(8,128)} async-done(((f32[8192,256]{1,0:T(8,128)}), f32[2048,256]{1,0:T(8,128)}) %reduce-scatter.30.cloned.1.call-update) | async-done | bytes 2097168 | tf_op jit(solution)/shard_map/reduce_scatter | solution.py:42
  (741 shorter events, 679.3 us)
Async XLA Ops:
  7.2 862.6 %copy-start = (bf16[256,704]{0,1:T(8,128)(2,1)S(1)}, bf16[256,704]{0,1:T(8,128)(2,1)}, u32[]{:S(2)}) copy-start(bf16[256,704]{0,1:T(8,128)(2,1)} %param.35) | copy-start | bytes 1081348
  7.2 95.2 %all-gather.15.cloned.1.call-start = ((), (), s32[]{:S(2)}) async-start(), calls=%async_computation.13 | async-start | bytes 5242880 | tf_op jit(solution)/shard_map/all_gather | solution.py:38
  21.2 116.6 %reduce-scatter.18.cloned.1.call-start = ((), (), s32[]{:S(2)}) async-start(), calls=%async_computation.16 | async-start | bytes 655360 | tf_op jit(solution)/shard_map/reduce_scatter | solution.py:177
  106.6 67.4 %reduce-scatter.16.cloned.1.call-start = ((), (), s32[]{:S(2)}) async-start(), calls=%async_computation.15 | async-start | bytes 5242880 | tf_op jit(solution)/shard_map/reduce_scatter | solution.py:173
  112.1 108.9 %reduce-scatter.20.cloned.1.call-start = ((), (), s32[]{:S(2)}) async-start(), calls=%async_computation.17 | async-start | bytes 5242880 | tf_op jit(solution)/shard_map/reduce_scatter | solution.py:174
  118.4 176.4 %reduce-scatter.14.cloned.1.call-start = ((), (), s32[]{:S(2)}) async-start(), calls=%async_computation.14 | async-start | bytes 10485760 | tf_op jit(solution)/shard_map/reduce_scatter | solution.py:175
  126.2 390.4 %reduce-scatter.22.cloned.1.call-start = ((), (), s32[]{:S(2)}) async-start(), calls=%async_computation.18 | async-start | bytes 10485760 | tf_op jit(solution)/shard_map/reduce_scatter | solution.py:176
  137.5 417.1 %all-gather.17.cloned.1.call-start = ((), (), s32[]{:S(2)}) async-start(), calls=%async_computation.19 | async-start | bytes 5242880 | tf_op jit(solution)/shard_map/all_gather | solution.py:191
  520.0 186.1 %reduce-scatter.24.cloned.1.call-start = ((), (), s32[]{:S(2)}) async-start(), calls=%async_computation.20 | async-start | bytes 10485760 | tf_op jit(solution)/shard_map/reduce_scatter | solution.py:42
  561.4 227.7 %all-gather.23.cloned.1.call-start = ((), (), s32[]{:S(2)}) async-start(), calls=%async_computation.26 | async-start | bytes 5242880 | tf_op jit(solution)/shard_map/all_gather | solution.py:38
  562.1 307.7 %all-gather.19.cloned.1.call-start = ((), (), s32[]{:S(2)}) async-start(), calls=%async_computation.21 | async-start | bytes 5242880 | tf_op jit(solution)/shard_map/all_gather | solution.py:38
  709.0 988.4 %copy-start.2 = (f32[2048,256]{1,0:T(8,128)}, f32[2048,256]{1,0:T(8,128)S(1)}, u32[]{:S(2)}) copy-start(f32[2048,256]{1,0:T(8,128)S(1)} %get-tuple-element.397) | copy-start | bytes 6291460
  719.3 314.6 %reduce-scatter.32.cloned.1.call-start = ((), (), s32[]{:S(2)}) async-start(), calls=%async_computation.27 | async-start | bytes 28835840 | tf_op jit(solution)/shard_map/reduce_scatter | solution.py:210
  803.2 396.2 %reduce-scatter.26.cloned.1.call-start = ((), (), s32[]{:S(2)}) async-start(), calls=%async_computation.22 | async-start | bytes 28835840 | tf_op jit(solution)/shard_map/reduce_scatter | solution.py:198
  886.4 478.6 %reduce-scatter.28.cloned.1.call-start = ((), (), s32[]{:S(2)}) async-start(), calls=%async_computation.23 | async-start | bytes 28835840 | tf_op jit(solution)/shard_map/reduce_scatter | solution.py:199
  903.4 548.7 %all-gather.25.cloned.1.call-start = ((), (), s32[]{:S(2)}) async-start(), calls=%async_computation.28 | async-start | bytes 14417920 | tf_op jit(solution)/shard_map/all_gather | solution.py:218
  1375.8 153.9 %all-gather.27.cloned.1.call-start = ((), (), s32[]{:S(2)}) async-start(), calls=%async_computation.29 | async-start | bytes 14417920 | tf_op jit(solution)/shard_map/all_gather | solution.py:219
  1376.4 311.7 %reduce-scatter.34.cloned.1.call-start = ((), (), s32[]{:S(2)}) async-start(), calls=%async_computation.30 | async-start | bytes 10485760 | tf_op jit(solution)/shard_map/reduce_scatter | solution.py:42
  1543.3 238.4 %all-gather.29.cloned.1.call-start = ((), (), s32[]{:S(2)}) async-start(), calls=%async_computation.31 | async-start | bytes 5242880 | tf_op jit(solution)/shard_map/all_gather | solution.py:38
  1700.4 130.0 %reduce-scatter.36.cloned.1.call-start = ((), (), s32[]{:S(2)}) async-start(), calls=%async_computation.32 | async-start | bytes 5242880 | tf_op jit(solution)/shard_map/reduce_scatter | solution.py:232
  1787.2 286.9 %all-gather.21.cloned.1.call-start = ((), (), s32[]{:S(2)}) async-start(), calls=%async_computation.24 | async-start | bytes 14417920 | tf_op jit(solution)/shard_map/all_gather | solution.py:203
  1788.0 298.0 %all-gather.39.cloned.1.call-start = ((), (), s32[]{:S(2)}) async-start(), calls=%async_computation.37 | async-start | bytes 2621440 | tf_op jit(solution)/shard_map/all_gather | solution.py:254
  2047.4 47.5 %all-gather.33.cloned.1.call-start = ((), (), s32[]{:S(2)}) async-start(), calls=%async_computation.34 | async-start | bytes 2621440 | tf_op jit(solution)/shard_map/all_gather | solution.py:251
  2048.1 71.5 %all-gather.31.cloned.1.call-start = ((), (), s32[]{:S(2)}) async-start(), calls=%async_computation.33 | async-start | bytes 2621440 | tf_op jit(solution)/shard_map/all_gather | solution.py:250
  2048.9 107.4 %all-gather.35.cloned.1.call-start = ((), (), s32[]{:S(2)}) async-start(), calls=%async_computation.35 | async-start | bytes 5242880 | tf_op jit(solution)/shard_map/all_gather | solution.py:252
  2056.7 136.0 %all-gather.37.cloned.1.call-start = ((), (), s32[]{:S(2)}) async-start(), calls=%async_computation.36 | async-start | bytes 5242880 | tf_op jit(solution)/shard_map/all_gather | solution.py:253
  2057.3 260.5 %all-reduce.6.cloned.1.call-start = ((), (), s32[]{:S(2)}) async-start(), calls=%async_computation.39 | async-start | bytes 131072 | tf_op jit(solution)/shard_map/psum | solution.py:343
  2092.8 280.8 %all-reduce.8.cloned.1.call-start = ((), (), s32[]{:S(2)}) async-start(), calls=%async_computation.40 | async-start | bytes 3080192 | tf_op jit(solution)/shard_map/psum | solution.py:49
  2198.2 322.3 %reduce-scatter.38.cloned.1.call-start = ((), (), s32[]{:S(2)}) async-start(), calls=%async_computation.38 | async-start | bytes 10485760 | tf_op jit(solution)/shard_map/reduce_scatter | solution.py:42
  2211.4 457.6 %reduce-scatter.30.cloned.1.call-start = ((), (), s32[]{:S(2)}) async-start(), calls=%async_computation.25 | async-start | bytes 10485760 | tf_op jit(solution)/shard_map/reduce_scatter | solution.py:42
  2234.2 434.8 %copy-start.3 = (f32[2048,256]{1,0:T(8,128)S(1)}, f32[2048,256]{1,0:T(8,128)}, u32[]{:S(2)}) copy-start(f32[2048,256]{1,0:T(8,128)} %copy-done.2) | copy-start | bytes 6291460
  2234.2 434.8 %copy-start.44 = (f32[2048]{0:T(1024)S(1)}, f32[2048]{0:T(1024)}, u32[]{:S(2)}) copy-start(f32[2048]{0:T(1024)} %copy-done.42) | copy-start | bytes 24580
  (71 other events, 3192.2 us)
Sparse Core Ops, SparseCore 0:
  21.3 81.0 all-gather.14
  106.7 20.1 reduce-scatter.17
  129.4 44.5 reduce-scatter.15
  176.4 44.5 reduce-scatter.19
  223.5 71.3 reduce-scatter.13
  297.3 71.3 reduce-scatter.21
  520.2 34.3 all-gather.16
  561.5 144.6 reduce-scatter.23
  707.7 81.3 all-gather.22
  790.5 79.2 all-gather.18
  872.4 161.4 reduce-scatter.31
  1036.4 162.9 reduce-scatter.25
  1202.0 162.9 reduce-scatter.27
  1375.9 76.1 all-gather.24
  1453.5 76.1 all-gather.26
  1543.4 144.6 reduce-scatter.33
  1700.6 81.1 all-gather.28
  1787.3 43.0 reduce-scatter.35
  1832.0 76.1 all-gather.20
  2047.5 22.5 all-gather.38
  2072.3 22.5 all-gather.32
  2097.0 22.5 all-gather.30
  2121.8 34.4 all-gather.34
  2158.2 34.4 all-gather.36
  2198.3 119.3 all-reduce.5
  2321.4 52.1 all-reduce.7
  2375.8 144.6 reduce-scatter.37
  2522.8 146.1 reduce-scatter.29
